TPU v7x, 256 devices: a whole 4x4x8 slice. The times are simulated.
256 devices in a mesh: gr: 16 (over z, core), gc: 16 (over x, y).
Axes of the slice: x: 4, y: 4, z: 8, core: 2. Of those that a mesh axis runs over, the one named last changes fastest.
Arguments:
- out_grad: bfloat16 [131072, 512], P(('gr', 'gc')), may hold values from -6 to 6
- preactivation_state: bfloat16 [131072, 512], P(('gr', 'gc')), may hold values from -6 to 6
- features: bfloat16 [131072, 512], P(('gc', 'gr')), may hold values from -24 to 24
- weight: bfloat16 [512, 512], replicated, may hold values from -0.25 to 0.25
- block_values: bfloat16 [16, 16, 152, 128, 128], P('gr', 'gc'), may hold values from -0.1875 to 0.1875
- block_rows: int32 [16, 16, 152], P('gr', 'gc'), may hold values from 0 to 63, as said below
- block_cols: int32 [16, 16, 152], P('gr', 'gc'), may hold values from 0 to 63, as said below
- block_counts: int32 [16, 16], P('gr', 'gc'), may hold values from 1 to 152, as said below
Outputs:
- input_grad: bfloat16 [131072, 512], P(('gc', 'gr'))
- weight_grad: float32 [512, 512], replicated
Inputs may be any that keep to these rules, and one draw needn't show every extreme that they name: `block_rows`: block row within a tile; some entry equals 63. `block_cols`: block column within a tile; some entry equals 63. `block_counts`: slots from this count on are unused; some tile uses all 152 slots.
All inputs are finite; a program needn't handle non-finite values.
Results may differ from a plain program's by a relative error of at most 0.014.
Values may be sent and summed in bfloat16 or wider, within the bound.
A program may use at most 128 MiB of HBM per device.

v0:
```python
import math
import jax
import jax.numpy as jnp
from jax import lax
from jax.sharding import PartitionSpec as P


def local(
    out_grad,
    preactivation_state,
    features,
    weight,
    block_values,
    block_rows,
    block_cols,
    block_counts,
):
    masked = jnp.where(preactivation_state > 0, out_grad, jnp.zeros_like(out_grad))
    tile_grads = lax.all_gather(masked, "gc", axis=0, tiled=True)
    block_size = block_values.shape[-1]
    feature_width = masked.shape[1]
    stacked = tile_grads.reshape(-1, block_size, feature_width)
    values_here = block_values[0, 0]
    rows_here = block_rows[0, 0]
    cols_here = block_cols[0, 0]
    count_here = block_counts[0, 0]
    capacity = values_here.shape[0]
    group_size = math.gcd(capacity, 16)
    node_rows = features.shape[0]
    col_count = node_rows * lax.axis_size("gr") // block_size

    def summing_group(current_index, value_partial_sum):
        offset = current_index * group_size
        current_values = lax.dynamic_slice_in_dim(values_here, offset, group_size, 0)
        rows_now = lax.dynamic_slice_in_dim(rows_here, offset, group_size, 0)
        cols_now = lax.dynamic_slice_in_dim(cols_here, offset, group_size, 0)
        selected_entries = stacked[rows_now]
        contribution = jnp.einsum(
            "yql,yqa->yla", current_values, selected_entries, preferred_element_type=jnp.float32
        )
        active = offset + jnp.arange(group_size) < count_here
        contribution = jnp.where(active[:, None, None], contribution, jnp.zeros_like(contribution))
        return value_partial_sum.at[cols_now].add(contribution)

    value_partial_sum = lax.fori_loop(
        0,
        capacity // group_size,
        summing_group,
        jnp.zeros((col_count, block_size, feature_width), jnp.float32),
    )
    value_partial_sum = value_partial_sum.reshape(-1, feature_width)
    column_total = lax.psum(value_partial_sum.astype(jnp.bfloat16), "gr").astype(jnp.float32)
    mine = lax.dynamic_slice_in_dim(column_total, lax.axis_index("gr") * node_rows, node_rows, 0)
    spread = mine.astype(jnp.bfloat16)
    input_grad = lax.dot_general(
        spread, weight, (((1,), (1,)), ((), ())), preferred_element_type=jnp.float32
    ).astype(jnp.bfloat16)
    weight_term = lax.dot_general(
        features, spread, (((0,), (0,)), ((), ())), preferred_element_type=jnp.float32
    )
    scale_factor = (node_rows * lax.axis_size("gr") * lax.axis_size("gc")) ** (-0.5)
    weight_grad = lax.psum(weight_term, ("gr", "gc")) * scale_factor
    return (input_grad, weight_grad)


def solution(mesh):
    in_specs = (
        P(("gr", "gc"), None),
        P(("gr", "gc"), None),
        P(("gc", "gr"), None),
        P(),
        P("gr", "gc", None, None, None),
        P("gr", "gc", None),
        P("gr", "gc", None),
        P("gr", "gc"),
    )
    out_specs = (P(("gc", "gr"), None), P())
    return jax.shard_map(local, mesh=mesh, in_specs=in_specs, out_specs=out_specs, check_vma=False)
```

profile of v0, /device:TPU:2, one launch (start us, length us, event | category | flops | bytes accessed | tf_op | source)
XLA Modules:
  0.0 739.5 jit_solution(15906717005274415228)
XLA Ops:
  9.4 7.7 %copy.10 = bf16[1,1,152,128,128]{3,4,2,1,0:T(8,128)(2,1)} copy(bf16[1,1,152,128,128]{4,3,2,1,0:T(8,128)(2,1)} %param.14) | data formatting | bytes 9961472 | tf_op args[4]
  17.1 72.7 %all-gather.2.cloned.1.call-done = bf16[8192,512]{1,0:T(8,128)(2,1)} async-done(((bf16[512,512]{1,0:T(8,128)(2,1)}), bf16[8192,512]{1,0:T(8,128)(2,1)}) %all-gather.2.cloned.1.call-update) | async-done | bytes 8388624 | tf_op jit(solution)/shard_map/all_gather | solution.py:19
  89.8 7.9 %broadcast_in_dim.38 = f32[64,128,512]{2,1,0:T(8,128)} broadcast(f32[]{:T(128)} %constant.51.clone.1), dimensions={} | broadcast | bytes 16777220 | tf_op jit(solution)/shard_map/broadcast_in_dim | solution.py:49
  97.7 224.4 %while.13 = (s32[]{:T(128)}, f32[64,128,512]{2,1,0:T(8,128)}, s32[152]{0:T(256)S(1)}, s32[]{:T(128)}, bf16[152,128,128]{1,2,0:T(8,128)(2,1)}, /*index=5*/s32[152...) while((s32[]{:T(128)}, f32[64,128,512]{2,1,0:T(8,128)}, ...), condition=%wide.region_2.3_spmd, body=%wide.region_0.2_spmd.sunk | while | flops 135267392 | bytes 11800995 | solution.py:45
  97.8 5.0 gather_fusion
  109.6 5.0 gather_fusion
  121.4 5.0 gather_fusion
  133.3 5.0 gather_fusion
  145.0 5.0 gather_fusion
  156.8 5.0 gather_fusion
  168.6 5.0 gather_fusion
  180.5 5.0 gather_fusion
  192.3 5.0 gather_fusion
  204.0 5.0 gather_fusion
  215.8 5.0 gather_fusion
  227.6 5.0 gather_fusion
  239.3 5.0 gather_fusion
  251.1 5.0 gather_fusion
  262.9 5.0 gather_fusion
  274.7 5.0 gather_fusion
  286.6 5.0 gather_fusion
  322.1 9.0 %convert_element_type.15 = bf16[64,128,512]{2,1,0:T(8,128)(2,1)} convert(f32[64,128,512]{2,1,0:T(8,128)} %get-tuple-element.126) | non-fusion elementwise | flops 4194304 | bytes 25165824 | tf_op jit(solution)/shard_map/convert_element_type | solution.py:52
  331.2 134.8 %all-reduce.3.cloned.1.call-done = bf16[8192,512]{1,0:T(8,128)(2,1)} async-done(((bf16[8192,512]{1,0:T(8,128)(2,1)}), bf16[8192,512]{1,0:T(8,128)(2,1)}) %all-reduce.3.cloned.1.call-update) | async-done | bytes 8388624 | tf_op jit(solution)/shard_map/psum | solution.py:52
  470.8 259.5 %all-reduce.5.cloned.1.call-done = f32[512,512]{0,1:T(8,128)} async-done(((f32[512,512]{0,1:T(8,128)}), f32[512,512]{0,1:T(8,128)}) %all-reduce.5.cloned.1.call-update) | async-done | bytes 1048592 | tf_op jit(solution)/shard_map/psum | solution.py:62
  (116 shorter events, 149.5 us)
Async XLA Ops:
  7.2 458.8 %copy-start = (bf16[512,512]{1,0:T(8,128)(2,1)S(1)}, bf16[512,512]{1,0:T(8,128)(2,1)}, u32[]{:S(2)}) copy-start(bf16[512,512]{1,0:T(8,128)(2,1)} %param.12) | copy-start | bytes 1572868
  7.2 82.6 %all-gather.2.cloned.1.call-start = ((), (), s32[]{:S(2)}) async-start(), calls=%async_computation | async-start | bytes 8912896 | tf_op jit(solution)/shard_map/all_gather | solution.py:19
  9.3 456.6 %all-reduce.3.cloned.1.call-start = ((), (), s32[]{:S(2)}) async-start(), calls=%async_computation.1 | async-start | bytes 16777216 | tf_op jit(solution)/shard_map/psum | solution.py:52
  89.8 7.9 %copy-start.2 = (s32[1,1,152]{2,1,0:T(1,128)S(1)}, s32[1,1,152]{2,1,0:T(1,128)}, u32[]{:S(2)}) copy-start(s32[1,1,152]{2,1,0:T(1,128)} %param.16) | copy-start | bytes 1828
  89.8 7.9 %copy-start.3 = (s32[1,1,152]{2,1,0:T(1,128)S(1)}, s32[1,1,152]{2,1,0:T(1,128)}, u32[]{:S(2)}) copy-start(s32[1,1,152]{2,1,0:T(1,128)} %param.15) | copy-start | bytes 1828
  331.1 137.4 %copy-start.1 = (bf16[512,512]{1,0:T(8,128)(2,1)S(1)}, bf16[512,512]{1,0:T(8,128)(2,1)}, u32[]{:S(2)}) copy-start(bf16[512,512]{1,0:T(8,128)(2,1)} %param.13) | copy-start | bytes 1572868
  331.1 399.2 %all-reduce.5.cloned.1.call-start = ((), (), s32[]{:S(2)}) async-start(), calls=%async_computation.2 | async-start | bytes 2097152 | tf_op jit(solution)/shard_map/psum | solution.py:62
Sparse Core Ops, SparseCore 0:
  11.0 78.7 all-gather.1
  331.2 134.7 all-reduce.2
  472.0 258.2 all-reduce.4
where the time goes:
time: 742 us; the launch traced here: 739 us
  waiting for transfers between devices  467 us (63%)
  local copies, waits for them, and re-layouts  111 us (15%)
  other arithmetic  109 us (15%)
  matrix products  37.8 us (5%)
  between operations  13.8 us (2%)
    psum x1, waiting for transfers between devices, local(): weight_grad = lax.psum(weight_term, ('gr', 'gc')) * scale_factor  260 us
    psum x1, waiting for transfers between devices, local(): lax.psum(value_partial_sum.astype(jnp.bfloat16), 'gr').astype(jnp.float32)  135 us
    gather x19, local copies, waits for them, and re-layouts, summing_group(): selected_entries = stacked[rows_now]  94.3 us
    scatter-add x19, other arithmetic, summing_group(): return value_partial_sum.at[cols_now].add(contribution)  82.9 us
    all_gather x1, waiting for transfers between devices, local(): tile_grads = lax.all_gather(masked, 'gc', axis=0, tiled=True)  72.7 us
    dot_general x19, matrix products, summing_group(): jnp.einsum('yql,yqa->yla', current_values, selected_entries, preferred_el...  33 us
  transfers between devices with their start and end apart: 3, of which 3 were waited for; matrix products, arithmetic and copies ran while one was open for 1% of the time, Pallas kernels for 0%

commit v1 on v0

--- a/solution.py
+++ b/solution.py
@@ -16,7 +16,9 @@
     block_counts,
 ):
     masked = jnp.where(preactivation_state > 0, out_grad, jnp.zeros_like(out_grad))
-    tile_grads = lax.all_gather(masked, "gc", axis=0, tiled=True)
+    tile_grads = jnp.concatenate(
+        lax.all_to_all(jnp.stack([masked] * lax.axis_size("gc")), "gc", 0, 0), axis=0
+    )
     block_size = block_values.shape[-1]
     feature_width = masked.shape[1]
     stacked = tile_grads.reshape(-1, block_size, feature_width)

time: 742 us -> 825 us (1.11)
  waiting for transfers between devices: 467 us -> 539 us
    all_to_all x0 -> x1, waiting for transfers between devices: none -> 97.1 us  [local(): lax.all_to_all(jnp.stack([masked] * lax.axis_size('gc')), 'gc', 0, 0)]
    all_gather x1 -> x0, waiting for transfers between devices: 72.7 us -> none  [local(): tile_grads = lax.all_gather(masked, 'gc', axis=0, tiled=True)]
    psum x1, waiting for transfers between devices: 135 us -> 182 us  [local(): lax.psum(value_partial_sum.astype(jnp.bfloat16), 'gr').astype(jnp.float32)]
where the time goes in v1:
time: 825 us; the launch traced here: 822 us
  waiting for transfers between devices  539 us (65%)
  local copies, waits for them, and re-layouts  115 us (14%)
  other arithmetic  108 us (13%)
  matrix products  37.8 us (5%)
  between operations  14.1 us (2%)
    psum x1, waiting for transfers between devices, local(): weight_grad = lax.psum(weight_term, ('gr', 'gc')) * scale_factor  259 us
    psum x1, waiting for transfers between devices, local(): lax.psum(value_partial_sum.astype(jnp.bfloat16), 'gr').astype(jnp.float32)  182 us
    all_to_all x1, waiting for transfers between devices, local(): lax.all_to_all(jnp.stack([masked] * lax.axis_size('gc')), 'gc', 0, 0)  97.1 us
    gather x19, local copies, waits for them, and re-layouts, summing_group(): selected_entries = stacked[rows_now]  94.3 us
    scatter-add x19, other arithmetic, summing_group(): return value_partial_sum.at[cols_now].add(contribution)  82.8 us
    dot_general x19, matrix products, summing_group(): jnp.einsum('yql,yqa->yla', current_values, selected_entries, preferred_el...  33 us
  transfers between devices with their start and end apart: 3, of which 3 were waited for; matrix products, arithmetic and copies ran while one was open for 1% of the time, Pallas kernels for 0%

profile of v1, /device:TPU:2, one launch (start us, length us, event | category | flops | bytes accessed | tf_op | source)
XLA Modules:
  0.0 822.1 jit_solution(1646732010114654779)
XLA Ops:
  12.5 7.5 all-to-all-start
  20.1 7.6 copy.10
  27.7 97.1 %all-to-all-done = bf16[16,512,512]{2,1,0:T(8,128)(2,1)} async-done(((bf16[16,512,512]{2,1,0:T(8,128)(2,1)}), bf16[16,512,512]{2,1,0:T(8,128)(2,1)}, u32[]{:S(2)}, u32[]{:S(2)}) %all-to-all-start) | async-done | bytes 8388640 | tf_op jit(solution)/shard_map/all_to_all | solution.py:20
  124.8 7.9 broadcast_in_dim.38
  132.7 224.3 %while.13 = (s32[]{:T(128)}, f32[64,128,512]{2,1,0:T(8,128)}, s32[152]{0:T(256)S(1)}, s32[]{:T(128)}, bf16[152,128,128]{1,2,0:T(8,128)(2,1)}, /*index=5*/s32[152...) while((s32[]{:T(128)}, f32[64,128,512]{2,1,0:T(8,128)}, ...), condition=%wide.region_2.3_spmd, body=%wide.region_0.2_spmd.sunk | while | flops 135267392 | bytes 11800995 | solution.py:47
  132.8 5.0 gather_fusion
  144.6 5.0 gather_fusion
  156.4 5.0 gather_fusion
  168.2 5.0 gather_fusion
  179.9 5.0 gather_fusion
  191.7 5.0 gather_fusion
  203.6 5.0 gather_fusion
  215.4 5.0 gather_fusion
  227.2 5.0 gather_fusion
  239.0 5.0 gather_fusion
  250.8 5.0 gather_fusion
  262.6 5.0 gather_fusion
  274.3 5.0 gather_fusion
  286.1 5.0 gather_fusion
  297.9 5.0 gather_fusion
  309.7 5.0 gather_fusion
  357.0 9.0 %convert_element_type.15 = bf16[64,128,512]{2,1,0:T(8,128)(2,1)} convert(f32[64,128,512]{2,1,0:T(8,128)} %get-tuple-element.126) | non-fusion elementwise | flops 4194304 | bytes 25165824 | tf_op jit(solution)/shard_map/convert_element_type | solution.py:54
  366.1 182.3 %all-reduce.3.cloned.1.call-done = bf16[8192,512]{1,0:T(8,128)(2,1)} async-done(((bf16[8192,512]{1,0:T(8,128)(2,1)}), bf16[8192,512]{1,0:T(8,128)(2,1)}) %all-reduce.3.cloned.1.call-update) | async-done | bytes 8388624 | tf_op jit(solution)/shard_map/psum | solution.py:54
  553.2 259.4 %all-reduce.5.cloned.1.call-done = f32[512,512]{0,1:T(8,128)} async-done(((f32[512,512]{0,1:T(8,128)}), f32[512,512]{0,1:T(8,128)}) %all-reduce.5.cloned.1.call-update) | async-done | bytes 1048592 | tf_op jit(solution)/shard_map/psum | solution.py:64
  (116 shorter events, 157.5 us)
Async XLA Ops:
  7.2 541.2 %copy-start = (bf16[512,512]{1,0:T(8,128)(2,1)S(1)}, bf16[512,512]{1,0:T(8,128)(2,1)}, u32[]{:S(2)}) copy-start(bf16[512,512]{1,0:T(8,128)(2,1)} %param.12) | copy-start | bytes 1572868
  12.5 112.3 %all-to-all-start = ((bf16[16,512,512]{2,1,0:T(8,128)(2,1)}), bf16[16,512,512]{2,1,0:T(8,128)(2,1)}, u32[]{:S(2)}, u32[]{:S(2)}) async-start(bf16[16,512,512]{2,1,0:T(8,128)(2,1)} %stack.2), calls=%async_computation | async-start | bytes 16777216 | tf_op jit(solution)/shard_map/all_to_all | solution.py:20
  20.0 528.3 %all-reduce.3.cloned.1.call-start = ((), (), s32[]{:S(2)}) async-start(), calls=%async_computation.1 | async-start | bytes 16777216 | tf_op jit(solution)/shard_map/psum | solution.py:54
  124.8 7.9 copy-start.2
  124.8 7.9 copy-start.3
  366.0 184.9 %copy-start.1 = (bf16[512,512]{1,0:T(8,128)(2,1)S(1)}, bf16[512,512]{1,0:T(8,128)(2,1)}, u32[]{:S(2)}) copy-start(bf16[512,512]{1,0:T(8,128)(2,1)} %param.13) | copy-start | bytes 1572868
  366.0 446.6 %all-reduce.5.cloned.1.call-start = ((), (), s32[]{:S(2)}) async-start(), calls=%async_computation.2 | async-start | bytes 2097152 | tf_op jit(solution)/shard_map/psum | solution.py:64
Sparse Core Ops, SparseCore 0:
  366.2 182.1 all-reduce.2
  554.4 258.2 all-reduce.4
